TPU v7x, 256 devices: a whole 4x4x8 slice. The times are simulated.
256 devices in a mesh: seq: 32 (over y, x, core), head: 8 (over z).
Axes of the slice: x: 4, y: 4, z: 8, core: 2. Of those that a mesh axis runs over, the one named last changes fastest.
Arguments:
- queries: bfloat16 [32768, 8192], P(('seq', 'head')), may hold values from -6 to 6
- key_vectors: bfloat16 [32768, 8192], P(('seq', 'head')), may hold values from -6 to 6
- value_vectors: bfloat16 [32768, 8192], P(('seq', 'head')), may hold values from -6 to 6
- out_gain: float32 [64, 128], P('head'), may hold values from 0.1 to 1.9
Outputs:
- attended: bfloat16 [32768, 8192], P(('seq', 'head'))
All inputs are finite; a program needn't handle non-finite values.
Results may differ from a plain program's by a relative error of at most 0.0049.
Values may be sent and summed in bfloat16 or wider, within the bound.
A program may use at most 128 MiB of HBM per device.

v0:
```python
import jax
import jax.numpy as jnp
from jax import lax
from jax.sharding import PartitionSpec as P

HEADS = 64
HD = 128


def shifted(block, axis, distance):
    count = lax.axis_size(axis)
    return lax.ppermute(block, axis, [(i, i + distance) for i in range(count - distance)])


def seq_exclusive(own):
    count = lax.axis_size("seq")
    total = own
    distance = 1
    while distance < count:
        total = total + shifted(total, "seq", distance)
        distance *= 2
    return shifted(total, "seq", 1)


def per_device(queries, key_vectors, value_vectors, out_gain):
    tokens = queries.shape[0]
    query_heads = queries.reshape(tokens, HEADS, HD)
    key_heads = key_vectors.reshape(tokens, HEADS, HD)
    value_heads = value_vectors.reshape(tokens, HEADS, HD)
    states = jnp.einsum("bhd,bhe->hde", key_heads, value_heads, preferred_element_type=jnp.float32)
    gathered = lax.all_to_all(
        states.astype(jnp.bfloat16).reshape(8, HEADS // 8, HD, HD),
        "head",
        split_axis=0,
        concat_axis=0,
        tiled=True,
    ).astype(jnp.float32)
    gain = lax.all_gather(out_gain, "head", axis=0, tiled=True)
    prefix = seq_exclusive(jnp.sum(gathered, axis=0))
    running = prefix
    parts = []
    for z in range(8):
        parts.append(running.astype(jnp.bfloat16))
        running = running + gathered[z]
    carried = lax.all_to_all(jnp.stack(parts), "head", split_axis=0, concat_axis=0, tiled=True)
    carried = carried.reshape(HEADS, HD, HD)
    inter = jnp.einsum("bhd,hde->bhe", query_heads, carried, preferred_element_type=jnp.float32)
    scores = jnp.einsum("bhd,chd->hbc", query_heads, key_heads, preferred_element_type=jnp.float32)
    causal = jnp.arange(tokens)[:, None] >= jnp.arange(tokens)[None, :]
    scores = jnp.where(causal[None], scores, jnp.float32(0.0)).astype(jnp.bfloat16)
    intra = jnp.einsum("hbc,chd->bhd", scores, value_heads, preferred_element_type=jnp.float32)
    raw = inter + intra
    scale = lax.rsqrt(jnp.mean(raw * raw, axis=-1, keepdims=True) + 1e-06)
    normed = (raw * scale * gain[None]).astype(jnp.bfloat16)
    return normed.reshape(tokens, HEADS * HD)


def solution(mesh):
    return jax.shard_map(
        per_device,
        mesh=mesh,
        in_specs=(
            P(("seq", "head"), None),
            P(("seq", "head"), None),
            P(("seq", "head"), None),
            P("head", None),
        ),
        out_specs=P(("seq", "head"), None),
        check_vma=False,
    )
```

profile of v0, /device:TPU:56, one launch (start us, length us, event | category | flops | bytes accessed | tf_op | source)
XLA Modules:
  0.0 247.2 jit_solution(813136822619654408)
XLA Ops:
  0.0 4.2 %copy.11 = bf16[128,8192]{0,1:T(8,128)(2,1)} copy(bf16[128,8192]{1,0:T(8,128)(2,1)} %param.5) | data formatting | bytes 4194304 | tf_op jit(solution)/shard_map/reshape | solution.py:28
  4.2 4.1 %copy.12 = bf16[128,8192]{0,1:T(8,128)(2,1)} copy(bf16[128,8192]{1,0:T(8,128)(2,1)} %param.6) | data formatting | bytes 4194304 | tf_op jit(solution)/shard_map/reshape | solution.py:29
  8.3 3.8 %convolution_convert_fusion = bf16[64,128,128]{2,1,0:T(8,128)(2,1)S(1)} fusion(bf16[128,64,128]{0,2,1:T(8,128)(2,1)} %bitcast.108, bf16[128,64,128]{0,2,1:T(8,128)(2,1)} %bitcast.110), kind=kOutput, calls=%fused_computation.7 | convolution fusion | flops 269484032 | bytes 6291456 | tf_op jit(solution)/shard_map/bhd,bhe->hde/dot_general | solution.py:30
  12.1 58.1 %all_to_all.10 = bf16[8,8,128,128]{3,2,1,0:T(8,128)(2,1)S(1)} all-to-all(bf16[8,8,128,128]{3,2,1,0:T(8,128)(2,1)S(1)} %bitcast.113), channel_id=1, replica_groups=mesh['seq'=32,'head'=8] {'head'}, dimensions={0} | all-to-all | bytes 4194304 | tf_op jit(solution)/shard_map/all_to_all | solution.py:31
  70.2 0.4 convert_reduce_fusion
  70.5 1.9 collective-permute-start
  72.5 10.7 %collective-permute-done = f32[8,128,128]{2,1,0:T(8,128)S(1)} collective-permute-done((f32[8,128,128]{2,1,0:T(8,128)S(1)}, f32[8,128,128]{2,1,0:T(8,128)S(1)}, u32[]{:S(2)}, u32[]{:S(2)}) %collective-permute-start) | collective-permute-done | bytes 524320 | tf_op jit(solution)/shard_map/ppermute | solution.py:12
  83.2 1.9 collective-permute-start.1
  85.1 12.9 %collective-permute-done.1 = f32[8,128,128]{2,1,0:T(8,128)S(1)} collective-permute-done((f32[8,128,128]{2,1,0:T(8,128)S(1)}, f32[8,128,128]{2,1,0:T(8,128)S(1)}, u32[]{:S(2)}, u32[]{:S(2)}) %collective-permute-start.1) | collective-permute-done | bytes 524320 | tf_op jit(solution)/shard_map/ppermute | solution.py:12
  98.1 2.5 %collective-permute-start.2 = (f32[8,128,128]{2,1,0:T(8,128)S(1)}, f32[8,128,128]{2,1,0:T(8,128)S(1)}, u32[]{:S(2)}, u32[]{:S(2)}) collective-permute-start(f32[8,128,128]{2,1,0:T(8,128)S(1)} %add.51), channel_id=1, source_target_pairs={{0,32},{8,40},{16,48},{24,56},{32,64},{40,72},{48,80},{56,88},{64,... | collective-permute-start | bytes 1572872 | tf_op jit(solution)/shard_map/ppermute | solution.py:12
  100.7 11.8 %collective-permute-done.2 = f32[8,128,128]{2,1,0:T(8,128)S(1)} collective-permute-done((f32[8,128,128]{2,1,0:T(8,128)S(1)}, f32[8,128,128]{2,1,0:T(8,128)S(1)}, u32[]{:S(2)}, u32[]{:S(2)}) %collective-permute-start.2) | collective-permute-done | bytes 524320 | tf_op jit(solution)/shard_map/ppermute | solution.py:12
  112.5 1.3 collective-permute-start.3
  113.8 9.9 %collective-permute-done.3 = f32[8,128,128]{2,1,0:T(8,128)S(1)} collective-permute-done((f32[8,128,128]{2,1,0:T(8,128)S(1)}, f32[8,128,128]{2,1,0:T(8,128)S(1)}, u32[]{:S(2)}, u32[]{:S(2)}) %collective-permute-start.3) | collective-permute-done | bytes 524320 | tf_op jit(solution)/shard_map/ppermute | solution.py:12
  123.7 1.3 collective-permute-start.4
  125.0 11.3 %collective-permute-done.4 = f32[8,128,128]{2,1,0:T(8,128)S(1)} collective-permute-done((f32[8,128,128]{2,1,0:T(8,128)S(1)}, f32[8,128,128]{2,1,0:T(8,128)S(1)}, u32[]{:S(2)}, u32[]{:S(2)}) %collective-permute-start.4) | collective-permute-done | bytes 524320 | tf_op jit(solution)/shard_map/ppermute | solution.py:12
  136.3 1.9 collective-permute-start.5
  138.3 0.5 convert_element_type.37
  138.8 10.2 %collective-permute-done.5 = f32[8,128,128]{2,1,0:T(8,128)S(1)} collective-permute-done((f32[8,128,128]{2,1,0:T(8,128)S(1)}, f32[8,128,128]{2,1,0:T(8,128)S(1)}, u32[]{:S(2)}, u32[]{:S(2)}) %collective-permute-start.5) | collective-permute-done | bytes 524320 | tf_op jit(solution)/shard_map/ppermute | solution.py:12
  149.0 0.7 bitcast_dynamic-update-slice_fusion.6
  149.7 0.8 bitcast_dynamic-update-slice_fusion.5
  150.4 0.8 bitcast_dynamic-update-slice_fusion.4
  151.2 0.8 bitcast_dynamic-update-slice_fusion.3
  152.0 0.8 bitcast_dynamic-update-slice_fusion.2
  152.8 0.8 bitcast_dynamic-update-slice_fusion.1
  153.6 0.8 bitcast_dynamic-update-slice_fusion
  154.4 0.8 fusion.16
  155.2 5.8 %all-to-all-start.1 = ((bf16[8,8,128,128]{3,2,1,0:T(8,128)(2,1)}), bf16[8,8,128,128]{3,2,1,0:T(8,128)(2,1)}, u32[]{:S(2)}, u32[]{:S(2)}) async-start(bf16[8,8,128,128]{3,2,1,0:T(8,128)(2,1)} %fusion.16), calls=%async_computation.1 | async-start | bytes 4194304 | tf_op jit(solution)/shard_map/all_to_all | solution.py:45
  161.0 65.5 %all_gather.3 = f32[64,128]{1,0:T(8,128)S(1)} all-gather(f32[8,128]{1,0:T(8,128)S(1)} %copy-done.1), channel_id=1, replica_groups=mesh['seq'=32,'head'=8] {'head'}, dimensions={0}, use_global_device_ids=true | all-gather | bytes 36864 | tf_op jit(solution)/shard_map/all_gather | solution.py:38
  226.5 5.1 %fusion.1 = f32[64,128,128]{2,1,0:T(8,128)} fusion(bf16[64,128,128]{2,1,0:T(8,128)(2,1)} %bitcast.21, bf16[128,8192]{1,0:T(8,128)(2,1)S(1)} %copy-done), kind=kOutput, calls=%fused_computation.5 | convolution fusion | flops 268435456 | bytes 8388608 | tf_op jit(solution)/shard_map/bhd,hde->bhe/dot_general | solution.py:47
  231.7 7.6 %multiply_reduce_fusion = (f32[128,64]{0,1:T(8,128)S(1)}, f32[128,64,128]{0,2,1:T(8,128)}) fusion(bf16[128,64,128]{0,2,1:T(8,128)(2,1)} %bitcast.111, bf16[128,64,128]{0,2,1:T(8,128)(2,1)} %bitcast.109, pred[128,128]{1,0:T(8,128)(4,1)S(1)} %iota_compare_fusion, f32[64,128,128]{2,1,0:T(8,128)} %fusion.1, bf16[128,8192]{1,0:T(8,128)(2,1)S(1)} %copy-done), kind=kOutput, calls=%fused_computation.2 | convolution fusion | flops 542105600 | bytes 14729216 | tf_op jit(solution)/shard_map/hbc,chd->bhd/dot_general | solution.py:51
  239.2 3.9 %multiply_convert_fusion = bf16[128,64,128]{0,2,1:T(8,128)(2,1)} fusion(f32[128,64,128]{0,2,1:T(8,128)} %get-tuple-element.10, f32[64,128]{1,0:T(8,128)S(1)} %all_gather.3, f32[128,64]{0,1:T(8,128)S(1)} %add_rsqrt_fusion), kind=kLoop, calls=%fused_computation.1 | loop fusion | flops 3145728 | bytes 6356992 | tf_op jit(solution)/shard_map/convert_element_type | solution.py:54
  243.1 4.1 %copy.10 = bf16[128,8192]{1,0:T(8,128)(2,1)} copy(bf16[128,8192]{0,1:T(8,128)(2,1)} %bitcast.112) | data formatting | bytes 4194304 | tf_op jit(solution)/shard_map/reshape | solution.py:55
  (12 shorter events, 0.3 us)
Async XLA Ops:
  0.0 226.5 %copy-start = (bf16[128,8192]{1,0:T(8,128)(2,1)S(1)}, bf16[128,8192]{1,0:T(8,128)(2,1)}, u32[]{:S(2)}) copy-start(bf16[128,8192]{1,0:T(8,128)(2,1)} %param.4) | copy-start | bytes 6291460
  70.5 12.6 %collective-permute-start = (f32[8,128,128]{2,1,0:T(8,128)S(1)}, f32[8,128,128]{2,1,0:T(8,128)S(1)}, u32[]{:S(2)}, u32[]{:S(2)}) collective-permute-start(f32[8,128,128]{2,1,0:T(8,128)S(1)} %convert_reduce_fusion), channel_id=1, source_target_pairs={{0,8},{8,16},{16,24},{24,32},{32,40},{40,48},{48,56},{56,64},{64,7... | collective-permute-start | bytes 1572872 | tf_op jit(solution)/shard_map/ppermute | solution.py:12
  83.2 14.8 %collective-permute-start.1 = (f32[8,128,128]{2,1,0:T(8,128)S(1)}, f32[8,128,128]{2,1,0:T(8,128)S(1)}, u32[]{:S(2)}, u32[]{:S(2)}) collective-permute-start(f32[8,128,128]{2,1,0:T(8,128)S(1)} %add.50), channel_id=1, source_target_pairs={{0,16},{8,24},{16,32},{24,40},{32,48},{40,56},{48,64},{56,72},{64,... | collective-permute-start | bytes 1572872 | tf_op jit(solution)/shard_map/ppermute | solution.py:12
  98.1 14.3 %collective-permute-start.2 = (f32[8,128,128]{2,1,0:T(8,128)S(1)}, f32[8,128,128]{2,1,0:T(8,128)S(1)}, u32[]{:S(2)}, u32[]{:S(2)}) collective-permute-start(f32[8,128,128]{2,1,0:T(8,128)S(1)} %add.51), channel_id=1, source_target_pairs={{0,32},{8,40},{16,48},{24,56},{32,64},{40,72},{48,80},{56,88},{64,... | collective-permute-start | bytes 1572872 | tf_op jit(solution)/shard_map/ppermute | solution.py:12
  112.5 11.2 %collective-permute-start.3 = (f32[8,128,128]{2,1,0:T(8,128)S(1)}, f32[8,128,128]{2,1,0:T(8,128)S(1)}, u32[]{:S(2)}, u32[]{:S(2)}) collective-permute-start(f32[8,128,128]{2,1,0:T(8,128)S(1)} %add.52), channel_id=1, source_target_pairs={{0,64},{8,72},{16,80},{24,88},{32,96},{40,104},{48,112},{56,120},{... | collective-permute-start | bytes 1572872 | tf_op jit(solution)/shard_map/ppermute | solution.py:12
  123.7 12.6 %collective-permute-start.4 = (f32[8,128,128]{2,1,0:T(8,128)S(1)}, f32[8,128,128]{2,1,0:T(8,128)S(1)}, u32[]{:S(2)}, u32[]{:S(2)}) collective-permute-start(f32[8,128,128]{2,1,0:T(8,128)S(1)} %add.53), channel_id=1, source_target_pairs={{0,128},{8,136},{16,144},{24,152},{32,160},{40,168},{48,176},{56,1... | collective-permute-start | bytes 1572872 | tf_op jit(solution)/shard_map/ppermute | solution.py:12
  136.3 12.6 %collective-permute-start.5 = (f32[8,128,128]{2,1,0:T(8,128)S(1)}, f32[8,128,128]{2,1,0:T(8,128)S(1)}, u32[]{:S(2)}, u32[]{:S(2)}) collective-permute-start(f32[8,128,128]{2,1,0:T(8,128)S(1)} %add.54), channel_id=1, source_target_pairs={{0,8},{8,16},{16,24},{24,32},{32,40},{40,48},{48,56},{56,64},{64,7... | collective-permute-start | bytes 1572872 | tf_op jit(solution)/shard_map/ppermute | solution.py:12
  155.2 5.8 %copy-start.1 = (f32[8,128]{1,0:T(8,128)S(1)}, f32[8,128]{1,0:T(8,128)}, u32[]{:S(2)}) copy-start(f32[8,128]{1,0:T(8,128)} %param.7) | copy-start | bytes 12292
  155.2 71.3 %all-to-all-start.1 = ((bf16[8,8,128,128]{3,2,1,0:T(8,128)(2,1)}), bf16[8,8,128,128]{3,2,1,0:T(8,128)(2,1)}, u32[]{:S(2)}, u32[]{:S(2)}) async-start(bf16[8,8,128,128]{3,2,1,0:T(8,128)(2,1)} %fusion.16), calls=%async_computation.1 | async-start | bytes 4194304 | tf_op jit(solution)/shard_map/all_to_all | solution.py:45
where the time goes:
time: 248 us; the launch traced here: 247 us
  blocking collectives  124 us (50%)
  waiting for transfers between devices  66.7 us (27%)
  starting transfers between devices  16.7 us (7%)
  matrix products  16.5 us (7%)
  local copies, waits for them, and re-layouts  12.3 us (5%)
  other arithmetic  11.3 us (5%)
    ppermute x6, waiting for transfers between devices, shifted(): lax.ppermute(block, axis, [(i, i + distance) for i in range(count - dista...  66.7 us
    all_gather x1, blocking collectives, per_device(): gain = lax.all_gather(out_gain, 'head', axis=0, tiled=True)  65.5 us
    all_to_all x1, blocking collectives, per_device(): lax.all_to_all(states.astype(jnp.bfloat16).reshape(8, HEADS // 8, HD, HD)...  58.1 us
    ppermute x6, starting transfers between devices, shifted(): lax.ppermute(block, axis, [(i, i + distance) for i in range(count - dista...  10.9 us
    dot_general x1, matrix products, per_device(): jnp.einsum('hbc,chd->bhd', scores, value_heads, preferred_element_type=jn...  7.56 us
    all_to_all x1, starting transfers between devices, per_device(): lax.all_to_all(jnp.stack(parts), 'head', split_axis=0, concat_axis=0, til...  5.8 us
    unnamed x7, other arithmetic  5.4 us
    dot_general x1, matrix products, per_device(): jnp.einsum('bhd,hde->bhe', query_heads, carried, preferred_element_type=j...  5.14 us
  transfers between devices with their start and end apart: 7, of which 6 were waited for; matrix products, arithmetic and copies ran while one was open for 0% of the time, Pallas kernels for 0%

commit v1 on v0

--- a/solution.py
+++ b/solution.py
@@ -1,10 +1,28 @@
+import functools
 import jax
 import jax.numpy as jnp
 from jax import lax
 from jax.sharding import PartitionSpec as P
+from jax.lax import axis_index, axis_size, ppermute
 
 HEADS = 64
 HD = 128
+
+
+def pieces_all_update(local_values, axis_tag):
+    amount_of = axis_size(axis_tag)
+    copies = [(kk, (kk + 1) % amount_of) for kk in range(amount_of)]
+    line_up = [(kk, (kk - 1) % amount_of) for kk in range(amount_of)]
+    val, piece_now = ([local_values], [local_values])
+    for _ in range(amount_of // 2):
+        val.append(ppermute(val[-1], axis_name=axis_tag, perm=copies))
+    for _ in range((amount_of - 1) // 2):
+        piece_now.append(ppermute(piece_now[-1], axis_tag, line_up))
+    built = jnp.concatenate([*val[::-1], *piece_now[1:]], 0)
+    return jnp.roll(built, (axis_index(axis_tag) - amount_of // 2) * local_values.shape[0], 0)
+
+
+draw_the_words = functools.partial(pieces_all_update, axis_tag="head")
 
 
 def shifted(block, axis, distance):
@@ -35,7 +53,7 @@
         concat_axis=0,
         tiled=True,
     ).astype(jnp.float32)
-    gain = lax.all_gather(out_gain, "head", axis=0, tiled=True)
+    gain = draw_the_words(out_gain)
     prefix = seq_exclusive(jnp.sum(gathered, axis=0))
     running = prefix
     parts = []

time: 248 us -> 244 us (0.984); the launches traced: 247 us -> 240 us
  blocking collectives: 124 us -> 58.1 us
  waiting for transfers between devices: 66.7 us -> 113 us
  starting transfers between devices: 16.7 us -> 28.3 us
    all_gather x1 -> x0, blocking collectives: 65.5 us -> none  [per_device(): gain = lax.all_gather(out_gain, 'head', axis=0, tiled=True)]
    ppermute x0 -> x7, waiting for transfers between devices: none -> 46.7 us  [the longest x4 44.6 us: pieces_all_update(): val.append(ppermute(val[-1], axis_name=axis_tag, perm=copies))]
    ppermute x0 -> x7, starting transfers between devices: none -> 11.6 us  [the longest x4 8.3 us: pieces_all_update(): val.append(ppermute(val[-1], axis_name=axis_tag, perm=copies))]
  transfers between devices with their start and end apart: 7 -> 14, of which waited for: 6 -> 13; matrix products, arithmetic and copies ran while one was open for 0% -> 0% of each run, Pallas kernels for 0% -> 0%
where the time goes in v1:
time: 244 us; the launch traced here: 240 us
  waiting for transfers between devices  113 us (46%)
  blocking collectives  58.1 us (24%)
  starting transfers between devices  28.3 us (12%)
  matrix products  16.5 us (7%)
  local copies, waits for them, and re-layouts  12.4 us (5%)
  other arithmetic  11.4 us (5%)
    ppermute x6, waiting for transfers between devices, shifted(): lax.ppermute(block, axis, [(i, i + distance) for i in range(count - dista...  66.7 us
    all_to_all x1, blocking collectives, per_device(): lax.all_to_all(states.astype(jnp.bfloat16).reshape(8, HEADS // 8, HD, HD)...  58.1 us
    ppermute x4, waiting for transfers between devices, pieces_all_update(): val.append(ppermute(val[-1], axis_name=axis_tag, perm=copies))  44.6 us
    ppermute x6, starting transfers between devices, shifted(): lax.ppermute(block, axis, [(i, i + distance) for i in range(count - dista...  10.9 us
    ppermute x4, starting transfers between devices, pieces_all_update(): val.append(ppermute(val[-1], axis_name=axis_tag, perm=copies))  8.3 us
    dot_general x1, matrix products, per_device(): jnp.einsum('hbc,chd->bhd', scores, value_heads, preferred_element_type=jn...  7.57 us
    all_to_all x1, starting transfers between devices, per_device(): lax.all_to_all(jnp.stack(parts), 'head', split_axis=0, concat_axis=0, til...  5.81 us
    unnamed x7, other arithmetic  5.53 us
  transfers between devices with their start and end apart: 14, of which 13 were waited for; matrix products, arithmetic and copies ran while one was open for 0% of the time, Pallas kernels for 0%

profile of v1, /device:TPU:56, one launch (start us, length us, event | category | flops | bytes accessed | tf_op | source)
XLA Modules:
  0.0 240.3 jit_solution(6923871710528606555)
XLA Ops:
  0.0 4.2 %copy.11 = bf16[128,8192]{0,1:T(8,128)(2,1)} copy(bf16[128,8192]{1,0:T(8,128)(2,1)} %param.5) | data formatting | bytes 4194304 | tf_op jit(solution)/shard_map/reshape | solution.py:46
  4.2 4.1 %copy.12 = bf16[128,8192]{0,1:T(8,128)(2,1)} copy(bf16[128,8192]{1,0:T(8,128)(2,1)} %param.6) | data formatting | bytes 4194304 | tf_op jit(solution)/shard_map/reshape | solution.py:47
  8.3 3.8 %convolution_convert_fusion = bf16[64,128,128]{2,1,0:T(8,128)(2,1)S(1)} fusion(bf16[128,64,128]{0,2,1:T(8,128)(2,1)} %bitcast.108, bf16[128,64,128]{0,2,1:T(8,128)(2,1)} %bitcast.110), kind=kOutput, calls=%fused_computation.7 | convolution fusion | flops 269484032 | bytes 6291456 | tf_op jit(solution)/shard_map/bhd,bhe->hde/dot_general | solution.py:48
  12.1 58.1 %all_to_all.10 = bf16[8,8,128,128]{3,2,1,0:T(8,128)(2,1)S(1)} all-to-all(bf16[8,8,128,128]{3,2,1,0:T(8,128)(2,1)S(1)} %bitcast.113), channel_id=1, replica_groups=mesh['seq'=32,'head'=8] {'head'}, dimensions={0} | all-to-all | bytes 4194304 | tf_op jit(solution)/shard_map/all_to_all | solution.py:49
  70.5 1.9 collective-permute-start
  72.5 10.7 %collective-permute-done = f32[8,128,128]{2,1,0:T(8,128)S(1)} collective-permute-done((f32[8,128,128]{2,1,0:T(8,128)S(1)}, f32[8,128,128]{2,1,0:T(8,128)S(1)}, u32[]{:S(2)}, u32[]{:S(2)}) %collective-permute-start) | collective-permute-done | bytes 524320 | tf_op jit(solution)/shard_map/ppermute | solution.py:30
  83.2 1.9 collective-permute-start.1
  85.1 12.9 %collective-permute-done.1 = f32[8,128,128]{2,1,0:T(8,128)S(1)} collective-permute-done((f32[8,128,128]{2,1,0:T(8,128)S(1)}, f32[8,128,128]{2,1,0:T(8,128)S(1)}, u32[]{:S(2)}, u32[]{:S(2)}) %collective-permute-start.1) | collective-permute-done | bytes 524320 | tf_op jit(solution)/shard_map/ppermute | solution.py:30
  98.1 2.5 %collective-permute-start.2 = (f32[8,128,128]{2,1,0:T(8,128)S(1)}, f32[8,128,128]{2,1,0:T(8,128)S(1)}, u32[]{:S(2)}, u32[]{:S(2)}) collective-permute-start(f32[8,128,128]{2,1,0:T(8,128)S(1)} %add.62), channel_id=1, source_target_pairs={{0,32},{8,40},{16,48},{24,56},{32,64},{40,72},{48,80},{56,88},{64,... | collective-permute-start | bytes 1572872 | tf_op jit(solution)/shard_map/ppermute | solution.py:30
  100.7 11.8 %collective-permute-done.2 = f32[8,128,128]{2,1,0:T(8,128)S(1)} collective-permute-done((f32[8,128,128]{2,1,0:T(8,128)S(1)}, f32[8,128,128]{2,1,0:T(8,128)S(1)}, u32[]{:S(2)}, u32[]{:S(2)}) %collective-permute-start.2) | collective-permute-done | bytes 524320 | tf_op jit(solution)/shard_map/ppermute | solution.py:30
  112.5 1.3 collective-permute-start.3
  113.8 9.9 %collective-permute-done.3 = f32[8,128,128]{2,1,0:T(8,128)S(1)} collective-permute-done((f32[8,128,128]{2,1,0:T(8,128)S(1)}, f32[8,128,128]{2,1,0:T(8,128)S(1)}, u32[]{:S(2)}, u32[]{:S(2)}) %collective-permute-start.3) | collective-permute-done | bytes 524320 | tf_op jit(solution)/shard_map/ppermute | solution.py:30
  123.7 1.3 collective-permute-start.4
  125.0 11.3 %collective-permute-done.4 = f32[8,128,128]{2,1,0:T(8,128)S(1)} collective-permute-done((f32[8,128,128]{2,1,0:T(8,128)S(1)}, f32[8,128,128]{2,1,0:T(8,128)S(1)}, u32[]{:S(2)}, u32[]{:S(2)}) %collective-permute-start.4) | collective-permute-done | bytes 524320 | tf_op jit(solution)/shard_map/ppermute | solution.py:30
  136.4 1.9 collective-permute-start.5
  138.8 10.2 %collective-permute-done.5 = f32[8,128,128]{2,1,0:T(8,128)S(1)} collective-permute-done((f32[8,128,128]{2,1,0:T(8,128)S(1)}, f32[8,128,128]{2,1,0:T(8,128)S(1)}, u32[]{:S(2)}, u32[]{:S(2)}) %collective-permute-start.5) | collective-permute-done | bytes 524320 | tf_op jit(solution)/shard_map/ppermute | solution.py:30
  155.4 5.8 %all-to-all-start.1 = ((bf16[8,8,128,128]{3,2,1,0:T(8,128)(2,1)}), bf16[8,8,128,128]{3,2,1,0:T(8,128)(2,1)}, u32[]{:S(2)}, u32[]{:S(2)}) async-start(bf16[8,8,128,128]{3,2,1,0:T(8,128)(2,1)} %fusion.16), calls=%async_computation.1 | async-start | bytes 4194304 | tf_op jit(solution)/shard_map/all_to_all | solution.py:63
  161.2 1.5 collective-permute-start.6
  162.6 40.4 %collective-permute-done.6 = f32[8,128]{1,0:T(8,128)S(1)} collective-permute-done((f32[8,128]{1,0:T(8,128)S(1)}, f32[8,128]{1,0:T(8,128)S(1)}, u32[]{:S(2)}, u32[]{:S(2)}) %collective-permute-start.6) | collective-permute-done | bytes 4128 | tf_op jit(solution)/shard_map/ppermute | solution.py:18
  203.0 3.1 %collective-permute-start.7 = (f32[8,128]{1,0:T(8,128)S(1)}, f32[8,128]{1,0:T(8,128)S(1)}, u32[]{:S(2)}, u32[]{:S(2)}) collective-permute-start(f32[8,128]{1,0:T(8,128)S(1)} %collective-permute-done.6), channel_id=1, source_target_pairs={{0,1},{1,2},{2,3},{3,4},{4,5},{5,6},{6,7},{7,0},{8,9},{9,10},{10,1... | collective-permute-start | bytes 12296 | tf_op jit(solution)/shard_map/ppermute | solution.py:18
  206.2 1.3 collective-permute-done.7
  207.5 2.6 %collective-permute-start.8 = (f32[8,128]{1,0:T(8,128)S(1)}, f32[8,128]{1,0:T(8,128)S(1)}, u32[]{:S(2)}, u32[]{:S(2)}) collective-permute-start(f32[8,128]{1,0:T(8,128)S(1)} %collective-permute-done.7), channel_id=1, source_target_pairs={{0,1},{1,2},{2,3},{3,4},{4,5},{5,6},{6,7},{7,0},{8,9},{9,10},{10,1... | collective-permute-start | bytes 12296 | tf_op jit(solution)/shard_map/ppermute | solution.py:18
  210.2 1.3 collective-permute-start.11
  211.5 1.6 collective-permute-done.8
  213.1 1.1 collective-permute-start.9
  214.7 2.0 collective-permute-start.12
  216.6 1.3 collective-permute-done.9
  217.9 1.6 collective-permute-done.12
  219.7 5.2 %fusion.1 = f32[64,128,128]{2,1,0:T(8,128)} fusion(bf16[64,128,128]{2,1,0:T(8,128)(2,1)} %bitcast.21, bf16[128,8192]{1,0:T(8,128)(2,1)S(1)} %copy-done), kind=kOutput, calls=%fused_computation.5 | convolution fusion | flops 268435456 | bytes 8388608 | tf_op jit(solution)/shard_map/bhd,hde->bhe/dot_general | solution.py:65
  224.8 7.6 %multiply_reduce_fusion = (f32[128,64]{0,1:T(8,128)S(1)}, f32[128,64,128]{0,2,1:T(8,128)}) fusion(bf16[128,64,128]{0,2,1:T(8,128)(2,1)} %bitcast.111, bf16[128,64,128]{0,2,1:T(8,128)(2,1)} %bitcast.109, pred[128,128]{1,0:T(8,128)(4,1)S(1)} %iota_compare_fusion, f32[64,128,128]{2,1,0:T(8,128)} %fusion.1, bf16[128,8192]{1,0:T(8,128)(2,1)S(1)} %copy-done), kind=kOutput, calls=%fused_computation.2 | convolution fusion | flops 542105600 | bytes 14729216 | tf_op jit(solution)/shard_map/hbc,chd->bhd/dot_general | solution.py:69
  232.4 3.9 %multiply_convert_fusion = bf16[128,64,128]{0,2,1:T(8,128)(2,1)} fusion(f32[128,64,128]{0,2,1:T(8,128)} %get-tuple-element.10, f32[64,128]{1,0:T(8,128)S(1)} %constant_dynamic-slice_fusion, f32[128,64]{0,1:T(8,128)S(1)} %add_rsqrt_fusion), kind=kLoop, calls=%fused_computation.1 | loop fusion | flops 3145728 | bytes 6356992 | tf_op jit(solution)/shard_map/convert_element_type | solution.py:72
  236.3 4.1 %copy.10 = bf16[128,8192]{1,0:T(8,128)(2,1)} copy(bf16[128,8192]{0,1:T(8,128)(2,1)} %bitcast.112) | data formatting | bytes 4194304 | tf_op jit(solution)/shard_map/reshape | solution.py:73
  (42 shorter events, 8.1 us)
Async XLA Ops:
  0.0 219.7 %copy-start = (bf16[128,8192]{1,0:T(8,128)(2,1)S(1)}, bf16[128,8192]{1,0:T(8,128)(2,1)}, u32[]{:S(2)}) copy-start(bf16[128,8192]{1,0:T(8,128)(2,1)} %param.4) | copy-start | bytes 6291460
  70.5 12.6 %collective-permute-start = (f32[8,128,128]{2,1,0:T(8,128)S(1)}, f32[8,128,128]{2,1,0:T(8,128)S(1)}, u32[]{:S(2)}, u32[]{:S(2)}) collective-permute-start(f32[8,128,128]{2,1,0:T(8,128)S(1)} %convert_reduce_fusion), channel_id=1, source_target_pairs={{0,8},{8,16},{16,24},{24,32},{32,40},{40,48},{48,56},{56,64},{64,7... | collective-permute-start | bytes 1572872 | tf_op jit(solution)/shard_map/ppermute | solution.py:30
  83.2 14.8 %collective-permute-start.1 = (f32[8,128,128]{2,1,0:T(8,128)S(1)}, f32[8,128,128]{2,1,0:T(8,128)S(1)}, u32[]{:S(2)}, u32[]{:S(2)}) collective-permute-start(f32[8,128,128]{2,1,0:T(8,128)S(1)} %add.61), channel_id=1, source_target_pairs={{0,16},{8,24},{16,32},{24,40},{32,48},{40,56},{48,64},{56,72},{64,... | collective-permute-start | bytes 1572872 | tf_op jit(solution)/shard_map/ppermute | solution.py:30
  98.1 14.3 %collective-permute-start.2 = (f32[8,128,128]{2,1,0:T(8,128)S(1)}, f32[8,128,128]{2,1,0:T(8,128)S(1)}, u32[]{:S(2)}, u32[]{:S(2)}) collective-permute-start(f32[8,128,128]{2,1,0:T(8,128)S(1)} %add.62), channel_id=1, source_target_pairs={{0,32},{8,40},{16,48},{24,56},{32,64},{40,72},{48,80},{56,88},{64,... | collective-permute-start | bytes 1572872 | tf_op jit(solution)/shard_map/ppermute | solution.py:30
  112.5 11.2 %collective-permute-start.3 = (f32[8,128,128]{2,1,0:T(8,128)S(1)}, f32[8,128,128]{2,1,0:T(8,128)S(1)}, u32[]{:S(2)}, u32[]{:S(2)}) collective-permute-start(f32[8,128,128]{2,1,0:T(8,128)S(1)} %add.63), channel_id=1, source_target_pairs={{0,64},{8,72},{16,80},{24,88},{32,96},{40,104},{48,112},{56,120},{... | collective-permute-start | bytes 1572872 | tf_op jit(solution)/shard_map/ppermute | solution.py:30
  123.7 12.6 %collective-permute-start.4 = (f32[8,128,128]{2,1,0:T(8,128)S(1)}, f32[8,128,128]{2,1,0:T(8,128)S(1)}, u32[]{:S(2)}, u32[]{:S(2)}) collective-permute-start(f32[8,128,128]{2,1,0:T(8,128)S(1)} %add.64), channel_id=1, source_target_pairs={{0,128},{8,136},{16,144},{24,152},{32,160},{40,168},{48,176},{56,1... | collective-permute-start | bytes 1572872 | tf_op jit(solution)/shard_map/ppermute | solution.py:30
  136.4 12.6 %collective-permute-start.5 = (f32[8,128,128]{2,1,0:T(8,128)S(1)}, f32[8,128,128]{2,1,0:T(8,128)S(1)}, u32[]{:S(2)}, u32[]{:S(2)}) collective-permute-start(f32[8,128,128]{2,1,0:T(8,128)S(1)} %add.65), channel_id=1, source_target_pairs={{0,8},{8,16},{16,24},{24,32},{32,40},{40,48},{48,56},{56,64},{64,7... | collective-permute-start | bytes 1572872 | tf_op jit(solution)/shard_map/ppermute | solution.py:30
  155.4 5.8 %copy-start.1 = (f32[8,128]{1,0:T(8,128)S(1)}, f32[8,128]{1,0:T(8,128)}, u32[]{:S(2)}) copy-start(f32[8,128]{1,0:T(8,128)} %param.7) | copy-start | bytes 12292
  155.4 64.3 %all-to-all-start.1 = ((bf16[8,8,128,128]{3,2,1,0:T(8,128)(2,1)}), bf16[8,8,128,128]{3,2,1,0:T(8,128)(2,1)}, u32[]{:S(2)}, u32[]{:S(2)}) async-start(bf16[8,8,128,128]{3,2,1,0:T(8,128)(2,1)} %fusion.16), calls=%async_computation.1 | async-start | bytes 4194304 | tf_op jit(solution)/shard_map/all_to_all | solution.py:63
  161.2 41.9 %collective-permute-start.6 = (f32[8,128]{1,0:T(8,128)S(1)}, f32[8,128]{1,0:T(8,128)S(1)}, u32[]{:S(2)}, u32[]{:S(2)}) collective-permute-start(f32[8,128]{1,0:T(8,128)S(1)} %copy-done.1), channel_id=1, source_target_pairs={{0,1},{1,2},{2,3},{3,4},{4,5},{5,6},{6,7},{7,0},{8,9},{9,10},{10,1... | collective-permute-start | bytes 12296 | tf_op jit(solution)/shard_map/ppermute | solution.py:18
  203.0 4.5 %collective-permute-start.7 = (f32[8,128]{1,0:T(8,128)S(1)}, f32[8,128]{1,0:T(8,128)S(1)}, u32[]{:S(2)}, u32[]{:S(2)}) collective-permute-start(f32[8,128]{1,0:T(8,128)S(1)} %collective-permute-done.6), channel_id=1, source_target_pairs={{0,1},{1,2},{2,3},{3,4},{4,5},{5,6},{6,7},{7,0},{8,9},{9,10},{10,1... | collective-permute-start | bytes 12296 | tf_op jit(solution)/shard_map/ppermute | solution.py:18
  206.2 4.0 %collective-permute-start.10 = (f32[8,128]{1,0:T(8,128)S(1)}, f32[8,128]{1,0:T(8,128)S(1)}, u32[]{:S(2)}, u32[]{:S(2)}) collective-permute-start(f32[8,128]{1,0:T(8,128)S(1)} %copy-done.1), channel_id=1, source_target_pairs={{0,7},{1,0},{2,1},{3,2},{4,3},{5,4},{6,5},{7,6},{8,15},{9,8},{10,9... | collective-permute-start | bytes 12296 | tf_op jit(solution)/shard_map/ppermute | solution.py:20
  207.5 5.6 %collective-permute-start.8 = (f32[8,128]{1,0:T(8,128)S(1)}, f32[8,128]{1,0:T(8,128)S(1)}, u32[]{:S(2)}, u32[]{:S(2)}) collective-permute-start(f32[8,128]{1,0:T(8,128)S(1)} %collective-permute-done.7), channel_id=1, source_target_pairs={{0,1},{1,2},{2,3},{3,4},{4,5},{5,6},{6,7},{7,0},{8,9},{9,10},{10,1... | collective-permute-start | bytes 12296 | tf_op jit(solution)/shard_map/ppermute | solution.py:18
  210.2 4.5 %collective-permute-start.11 = (f32[8,128]{1,0:T(8,128)S(1)}, f32[8,128]{1,0:T(8,128)S(1)}, u32[]{:S(2)}, u32[]{:S(2)}) collective-permute-start(f32[8,128]{1,0:T(8,128)S(1)} %collective-permute-done.10), channel_id=1, source_target_pairs={{0,7},{1,0},{2,1},{3,2},{4,3},{5,4},{6,5},{7,6},{8,15},{9,8},{10,9... | collective-permute-start | bytes 12296 | tf_op jit(solution)/shard_map/ppermute | solution.py:20
  213.1 4.8 %collective-permute-start.9 = (f32[8,128]{1,0:T(8,128)S(1)}, f32[8,128]{1,0:T(8,128)S(1)}, u32[]{:S(2)}, u32[]{:S(2)}) collective-permute-start(f32[8,128]{1,0:T(8,128)S(1)} %collective-permute-done.8), channel_id=1, source_target_pairs={{0,1},{1,2},{2,3},{3,4},{4,5},{5,6},{6,7},{7,0},{8,9},{9,10},{10,1... | collective-permute-start | bytes 12296 | tf_op jit(solution)/shard_map/ppermute | solution.py:18
  214.7 4.9 %collective-permute-start.12 = (f32[8,128]{1,0:T(8,128)S(1)}, f32[8,128]{1,0:T(8,128)S(1)}, u32[]{:S(2)}, u32[]{:S(2)}) collective-permute-start(f32[8,128]{1,0:T(8,128)S(1)} %collective-permute-done.11), channel_id=1, source_target_pairs={{0,7},{1,0},{2,1},{3,2},{4,3},{5,4},{6,5},{7,6},{8,15},{9,8},{10,9... | collective-permute-start | bytes 12296 | tf_op jit(solution)/shard_map/ppermute | solution.py:20
